TPU v7x, 32 devices: a whole 2x2x4 slice. The times are simulated.
32 devices in a mesh: fsdp: 8 (over z, y), tp: 4 (over x, core).
Axes of the slice: x: 2, y: 2, z: 4, core: 2. Of those that a mesh axis runs over, the one named last changes fastest.
Arguments:
- states: bfloat16 [8, 8, 32, 4096], P('fsdp', None, None, 'tp'), may hold values from -40 to 40
- dest: int32 [8, 8], P('fsdp'), may hold values from 0 to 7, each once within a row
- lengths: int32 [8, 8], P('fsdp'), may hold values from 1 to 32, 160 in all within a row
- strata: int32 [8, 8, 1], P('fsdp'), may hold values from 0 to 7
- ffn_gain: float32 [4096], replicated, may hold values from 0.1 to 1.9
- gate_weight: bfloat16 [4096, 7168], P('fsdp', 'tp'), may hold values from -0.0703125 to 0.0703125
- up_weight: bfloat16 [4096, 7168], P('fsdp', 'tp'), may hold values from -0.1 to 0.1
- down_weight: bfloat16 [7168, 4096], P('tp', 'fsdp'), may hold values from -0.058238643 to 0.058238643
- final_gain: float32 [4096], replicated, may hold values from 0.1 to 1.9
- value_weight: float32 [4096], replicated, may hold values from -0.09375 to 0.09375
Outputs:
- rewards: float32 [8, 8], P('fsdp')
- stratum_means: float32 [8], replicated
Inputs may be any that keep to these rules, and one draw needn't show every extreme that they name: Each row of dest is a permutation: every source group sends exactly one response to every scoring group. Each source group's lengths sum to 160. `strata`: every stratum holds at least one response.
All inputs are finite; a program needn't handle non-finite values.
Results may differ from a plain program's by a relative error of at most 0.004.
Values may be sent and summed in bfloat16 or wider, within the bound.
A program may use at most 128 MiB of HBM per device.

v0:
```python
import jax
import jax.numpy as jnp
from jax import lax
from jax.sharding import PartitionSpec as P

S = 8
epsilon = 1e-05


def body(
    states,
    dest,
    lengths,
    strata,
    ffn_gain,
    gate_weight,
    up_weight,
    down_weight,
    final_gain,
    value_weight,
):
    groups = dest.shape[1]
    length = states.shape[2]
    slots = jnp.arange(groups, dtype=jnp.int32)
    picker = (dest[0][None, :] == slots[:, None]).astype(jnp.int32)
    source_slot = jnp.sum(picker * slots[None, :], axis=1)
    outgoing = jnp.take(states[0], source_slot, axis=0)
    out_len = jnp.take(lengths[0], source_slot, axis=0)
    out_str = jnp.take(strata[0, :, 0], source_slot, axis=0)
    received, recv_len, recv_str = (
        lax.all_to_all(outgoing, "fsdp", split_axis=0, concat_axis=0, tiled=True),
        lax.all_to_all(out_len, "fsdp", split_axis=0, concat_axis=0, tiled=True),
        lax.all_to_all(out_str, "fsdp", split_axis=0, concat_axis=0, tiled=True),
    )
    gathered = lax.all_gather(received, "tp", axis=2, tiled=True)
    feature_width = gathered.shape[2]
    token_count = groups * length
    widened = gathered.reshape(token_count, feature_width).astype(jnp.float32)
    normed = (
        widened
        * lax.rsqrt(jnp.mean(widened * widened, axis=1, keepdims=True) + epsilon)
        * ffn_gain[None, :]
    ).astype(jnp.bfloat16)
    gate_full, up_full, down_full = (
        lax.all_gather(gate_weight, "fsdp", axis=0, tiled=True),
        lax.all_gather(up_weight, "fsdp", axis=0, tiled=True),
        lax.all_gather(down_weight, "fsdp", axis=1, tiled=True),
    )
    gate = jnp.dot(normed, gate_full, preferred_element_type=jnp.float32)
    up_part = jnp.dot(normed, up_full, preferred_element_type=jnp.float32)
    hidden = (jax.nn.silu(gate) * up_part).astype(jnp.bfloat16)
    partial_value = jnp.dot(hidden, down_full, preferred_element_type=jnp.float32)
    head_scale = final_gain * value_weight
    total = lax.psum(partial_value.astype(jnp.bfloat16), "tp").astype(jnp.float32)
    mixed = widened + total
    product = jnp.sum(mixed * head_scale[None, :], axis=1)
    value = product * lax.rsqrt(jnp.mean(mixed * mixed, axis=1) + epsilon)
    value = value.reshape(groups, length)
    positions = jnp.arange(length, dtype=jnp.int32)
    live_mask = (positions[None, :] < recv_len[:, None]).astype(jnp.float32)
    reward = jnp.sum(value * live_mask, axis=1) / recv_len.astype(jnp.float32)
    strata_ids = jnp.arange(S, dtype=jnp.int32)
    onehot = (recv_str[:, None] == strata_ids[None, :]).astype(jnp.float32)
    sums = jnp.sum(reward[:, None] * onehot, axis=0)
    counts = jnp.sum(onehot, axis=0)
    sums, counts = lax.psum((sums, counts), "fsdp")
    return (reward.reshape(1, groups), sums / counts)


def solution(mesh):
    return jax.shard_map(
        body,
        mesh=mesh,
        in_specs=(
            P("fsdp", None, None, "tp"),
            P("fsdp", None),
            P("fsdp", None),
            P("fsdp", None, None),
            P(),
            P("fsdp", "tp"),
            P("fsdp", "tp"),
            P("tp", "fsdp"),
            P(),
            P(),
        ),
        out_specs=(P("fsdp", None), P()),
        check_vma=False,
    )
```

profile of v0, /device:TPU:0, one launch (start us, length us, event | category | flops | bytes accessed | tf_op | source)
XLA Modules:
  0.0 764.5 jit_solution(11980279169275734645)
XLA Ops:
  7.2 0.0 copy-start
  7.2 0.0 all-gather.5.cloned.1.call-start
  7.2 0.8 select_reduce_fusion.2
  8.1 1.3 gather_fusion.2
  9.4 0.0 copy-done
  9.4 0.6 gather_fusion
  10.0 0.1 broadcast_select_fusion
  10.1 21.7 %all_to_all.23 = bf16[8,32,1024]{2,1,0:T(8,128)(2,1)} all-to-all(bf16[8,32,1024]{2,1,0:T(8,128)(2,1)S(1)} %broadcast_select_fusion), channel_id=1, replica_groups=mesh['fsdp'=8,'tp'=4] {'fsdp'}, dimensions={0} | all-to-all | bytes 1048576 | tf_op jit(solution)/shard_map/all_to_all | solution.py:31
  31.8 0.0 all-gather.5.cloned.1.call-update
  31.9 0.0 all-gather.7.cloned.1.call-start
  31.9 0.7 all-gather.7.cloned.1.call-update
  32.6 0.0 all-gather.11.cloned.1.call-start
  32.7 0.7 all-gather.11.cloned.1.call-update
  33.3 0.0 copy-start.3
  33.4 0.0 all-gather.9.cloned.1.call-start
  33.4 0.5 all-gather.9.cloned.1.call-update
  33.9 0.0 all-reduce.3.cloned.1.call-start
  34.0 19.6 %all-gather.5.cloned.1.call-done = bf16[8,32,4096]{2,1,0:T(8,128)(2,1)} async-done(((bf16[8,32,1024]{2,1,0:T(8,128)(2,1)}), bf16[8,32,4096]{2,1,0:T(8,128)(2,1)}) %all-gather.5.cloned.1.call-update) | async-done | bytes 2097168 | tf_op jit(solution)/shard_map/all_gather | solution.py:35
  53.6 0.0 copy-start.2
  53.6 2.2 fusion
  55.8 0.1 rsqrt.17
  55.9 0.0 copy-done.3
  55.9 0.0 copy-done.2
  55.9 1.9 fusion.2
  57.9 200.0 %all-gather.7.cloned.1.call-done = bf16[4096,1792]{1,0:T(8,128)(2,1)} async-done(((bf16[512,1792]{1,0:T(8,128)(2,1)}), bf16[4096,1792]{1,0:T(8,128)(2,1)}) %all-gather.7.cloned.1.call-update) | async-done | bytes 14680080 | tf_op jit(solution)/shard_map/all_gather | solution.py:45
  257.8 11.0 %fusion.6 = f32[256,1792]{1,0:T(8,128)} fusion(bf16[256,4096]{1,0:T(8,128)(2,1)} %fusion.2, bf16[4096,1792]{1,0:T(8,128)(2,1)} %all-gather.7.cloned.1.call-done), kind=kOutput, calls=%fused_computation.36 | convolution fusion | flops 3758096384 | bytes 18612224 | tf_op jit(solution)/shard_map/dot_general | solution.py:49
  268.9 191.5 %all-gather.11.cloned.1.call-done = bf16[1792,4096]{1,0:T(8,128)(2,1)} async-done(((bf16[1792,512]{1,0:T(8,128)(2,1)}), bf16[1792,4096]{1,0:T(8,128)(2,1)}) %all-gather.11.cloned.1.call-update) | async-done | bytes 14680080 | tf_op jit(solution)/shard_map/all_gather | solution.py:47
  460.4 202.3 %all-gather.9.cloned.1.call-done = bf16[4096,1792]{1,0:T(8,128)(2,1)} async-done(((bf16[512,1792]{1,0:T(8,128)(2,1)}), bf16[4096,1792]{1,0:T(8,128)(2,1)}) %all-gather.9.cloned.1.call-update) | async-done | bytes 14680080 | tf_op jit(solution)/shard_map/all_gather | solution.py:46
  662.6 20.2 %convolution_convert_fusion = bf16[256,4096]{1,0:T(8,128)(2,1)} fusion(bf16[1792,4096]{1,0:T(8,128)(2,1)} %all-gather.11.cloned.1.call-done, bf16[256,4096]{1,0:T(8,128)(2,1)} %fusion.2, bf16[4096,1792]{1,0:T(8,128)(2,1)} %all-gather.9.cloned.1.call-done, f32[256,1792]{1,0:T(8,128)} %fusion.6), kind=kOutput, calls=%fused_computation.3 | convolution fusion | flops 7519993856 | bytes 35389440 | tf_op jit(solution)/shard_map/dot_general | solution.py:52
  682.8 0.0 copy-start.1
  682.8 0.0 copy-start.4
  682.8 0.0 copy-start.5
  682.8 0.0 all-reduce.3.cloned.1.call-update
  682.8 0.6 copy-done.1
  683.4 0.6 gather_fusion.1
  684.1 0.7 copy.16
  684.8 3.3 all-to-all-start
  688.0 0.7 copy.17
  688.7 0.0 copy-done.4
  688.7 0.0 copy-done.5
  688.7 5.7 all-to-all-done
  694.4 3.3 all-to-all-start.2
  697.7 0.2 reduce.1
  698.0 6.2 all-to-all-done.2
  704.1 0.2 reduce.3
  704.4 0.1 convert_reduce_fusion.1
  704.5 28.0 %all-reduce.3.cloned.1.call-done = bf16[256,4096]{1,0:T(8,128)(2,1)} async-done(((bf16[256,4096]{1,0:T(8,128)(2,1)}), bf16[256,4096]{1,0:T(8,128)(2,1)}) %all-reduce.3.cloned.1.call-update) | async-done | bytes 2097168 | tf_op jit(solution)/shard_map/psum | solution.py:54
  732.5 2.7 multiply_reduce_fusion
  735.2 0.1 mul.83
  735.3 0.2 select_reduce_fusion.1
  735.5 0.5 bitcast_divide_fusion
  736.0 0.1 convert_reduce_fusion
  736.1 21.4 %all-reduce = (f32[8]{0:T(128)S(1)}, f32[8]{0:T(128)S(1)}) all-reduce(f32[8]{0:T(128)S(1)} %get-tuple-element.6, f32[8]{0:T(128)S(1)} %get-tuple-element.5), channel_id=1, replica_groups=mesh['fsdp'=8,'tp'=4] {'fsdp'}, use_global_device_ids=true, to_apply=%region_7.9 | all-reduce | flops 16 | bytes 128 | tf_op jit(solution)/shard_map/psum | solution.py:66
  757.5 0.5 div.42
  (10 shorter events, 0.1 us)
Async XLA Ops:
  7.2 2.2 copy-start
  7.2 46.4 %all-gather.5.cloned.1.call-start = ((), (), s32[]{:S(2)}) async-start(), calls=%async_computation.3 | async-start | bytes 2621440 | tf_op jit(solution)/shard_map/all_gather | solution.py:35
  31.9 226.0 %all-gather.7.cloned.1.call-start = ((), (), s32[]{:S(2)}) async-start(), calls=%async_computation.4 | async-start | bytes 16515072 | tf_op jit(solution)/shard_map/all_gather | solution.py:45
  32.6 427.7 %all-gather.11.cloned.1.call-start = ((), (), s32[]{:S(2)}) async-start(), calls=%async_computation.6 | async-start | bytes 16515072 | tf_op jit(solution)/shard_map/all_gather | solution.py:47
  33.3 22.6 %copy-start.3 = (f32[4096]{0:T(1024)S(1)}, f32[4096]{0:T(1024)}, u32[]{:S(2)}) copy-start(f32[4096]{0:T(1024)} %param.16) | copy-start | bytes 49156
  33.4 629.3 %all-gather.9.cloned.1.call-start = ((), (), s32[]{:S(2)}) async-start(), calls=%async_computation.5 | async-start | bytes 16515072 | tf_op jit(solution)/shard_map/all_gather | solution.py:46
  33.9 698.6 %all-reduce.3.cloned.1.call-start = ((), (), s32[]{:S(2)}) async-start(), calls=%async_computation.7 | async-start | bytes 4194304 | tf_op jit(solution)/shard_map/psum | solution.py:54
  53.6 2.3 copy-start.2
  682.8 0.7 copy-start.1
  682.8 5.9 copy-start.4
  682.8 5.9 copy-start.5
  684.8 9.7 %all-to-all-start = ((s32[8,1,1]{2,1,0:T(1,128)}), s32[8,1,1]{2,1,0:T(1,128)S(1)}, u32[]{:S(2)}, u32[]{:S(2)}) async-start(s32[8,1,1]{2,1,0:T(1,128)} %copy.16), calls=%async_computation | async-start | bytes 8192 | tf_op jit(solution)/shard_map/all_to_all | solution.py:32
  694.4 9.7 %all-to-all-start.2 = ((s32[8,1,1]{2,1,0:T(1,128)}), s32[8,1,1]{2,1,0:T(1,128)S(1)}, u32[]{:S(2)}, u32[]{:S(2)}) async-start(s32[8,1,1]{2,1,0:T(1,128)} %copy.17), calls=%async_computation.2 | async-start | bytes 8192 | tf_op jit(solution)/shard_map/all_to_all | solution.py:33
Sparse Core Ops, SparseCore 0:
  32.0 21.5 all-gather.4
  55.8 202.0 all-gather.6
  259.9 200.4 all-gather.10
  462.4 200.1 all-gather.8
  682.9 49.5 all-reduce.2
where the time goes:
time: 765 us
  waiting for transfers between devices  655 us (86%)
  blocking collectives  43.1 us (6%)
  matrix products  31.2 us (4%)
  between operations  13.9 us (2%)
  other arithmetic  9.75 us (1%)
    all_gather x1, waiting for transfers between devices, body(): lax.all_gather(up_weight, 'fsdp', axis=0, tiled=True)  202 us
    all_gather x1, waiting for transfers between devices, body(): lax.all_gather(gate_weight, 'fsdp', axis=0, tiled=True)  200 us
    all_gather x1, waiting for transfers between devices, body(): lax.all_gather(down_weight, 'fsdp', axis=1, tiled=True)  192 us
    psum x1, waiting for transfers between devices, body(): lax.psum(partial_value.astype(jnp.bfloat16), 'tp').astype(jnp.float32)  28 us
    all_to_all x1, blocking collectives, body(): lax.all_to_all(outgoing, 'fsdp', split_axis=0, concat_axis=0, tiled=True)  21.7 us
    psum x1, blocking collectives, body(): sums, counts = lax.psum((sums, counts), 'fsdp')  21.4 us
    dot_general x1, matrix products, body(): jnp.dot(hidden, down_full, preferred_element_type=jnp.float32)  20.2 us
    all_gather x1, waiting for transfers between devices, body(): gathered = lax.all_gather(received, 'tp', axis=2, tiled=True)  19.6 us
  transfers between devices with their start and end apart: 7, of which 7 were waited for; matrix products, arithmetic and copies ran while one was open for 2% of the time, Pallas kernels for 0%

commit v1 on v0

--- a/solution.py
+++ b/solution.py
@@ -1,10 +1,28 @@
+import functools
 import jax
 import jax.numpy as jnp
 from jax import lax
 from jax.sharding import PartitionSpec as P
+from jax.lax import axis_index, axis_size, ppermute
 
 S = 8
 epsilon = 1e-05
+
+
+def mix_squares_over_axis(vec, mesh_ax):
+    n = axis_size(mesh_ax)
+    cards = [vec]
+    for u in range(n - 1):
+        mid_arr = ppermute(
+            cards[-1], axis_name=mesh_ax, perm=[(dev_j, (dev_j + 1) % n) for dev_j in range(n)]
+        )
+        cards.append(mid_arr)
+    current_value = jnp.concatenate(cards[::-1], axis=2)
+    plain = axis_index(mesh_ax)
+    return jnp.roll(current_value, (plain + 1) * vec.shape[2], axis=2)
+
+
+_settle_kinds = functools.partial(mix_squares_over_axis, mesh_ax="tp")
 
 
 def body(
@@ -32,7 +50,7 @@
         lax.all_to_all(out_len, "fsdp", split_axis=0, concat_axis=0, tiled=True),
         lax.all_to_all(out_str, "fsdp", split_axis=0, concat_axis=0, tiled=True),
     )
-    gathered = lax.all_gather(received, "tp", axis=2, tiled=True)
+    gathered = _settle_kinds(received)
     feature_width = gathered.shape[2]
     token_count = groups * length
     widened = gathered.reshape(token_count, feature_width).astype(jnp.float32)

time: 765 us -> 728 us (0.952)
  waiting for transfers between devices: 655 us -> 610 us
  blocking collectives: 43.1 us -> 54.5 us
    all_gather x1, waiting for transfers between devices: 200 us -> 146 us  [body(): lax.all_gather(gate_weight, 'fsdp', axis=0, tiled=True)]
    ppermute x0 -> x3, waiting for transfers between devices: none -> 25.8 us  [mix_squares_over_axis(): ppermute(cards[-1], axis_name=mesh_ax, perm=[(dev_j, (dev_j + 1) % n) for...]
    all_gather x1 -> x0, waiting for transfers between devices: 19.6 us -> none  [body(): gathered = lax.all_gather(received, 'tp', axis=2, tiled=True)]
    all_to_all x1, blocking collectives: 21.7 us -> 33.1 us  [body(): lax.all_to_all(outgoing, 'fsdp', split_axis=0, concat_axis=0, tiled=True)]
    all_gather x1, waiting for transfers between devices: 192 us -> 202 us  [body(): lax.all_gather(down_weight, 'fsdp', axis=1, tiled=True)]
    all_gather x1, waiting for transfers between devices: 202 us -> 194 us  [body(): lax.all_gather(up_weight, 'fsdp', axis=0, tiled=True)]
  transfers between devices with their start and end apart: 7 -> 9, of which waited for: 7 -> 9; matrix products, arithmetic and copies ran while one was open for 2% -> 2% of each run, Pallas kernels for 0% -> 0%
where the time goes in v1:
time: 728 us
  waiting for transfers between devices  610 us (84%)
  blocking collectives  54.5 us (7%)
  matrix products  28.1 us (4%)
  between operations  14 us (2%)
  other arithmetic  8.21 us (1%)
    all_gather x1, waiting for transfers between devices, body(): lax.all_gather(down_weight, 'fsdp', axis=1, tiled=True)  202 us
    all_gather x1, waiting for transfers between devices, body(): lax.all_gather(up_weight, 'fsdp', axis=0, tiled=True)  194 us
    all_gather x1, waiting for transfers between devices, body(): lax.all_gather(gate_weight, 'fsdp', axis=0, tiled=True)  146 us
    all_to_all x1, blocking collectives, body(): lax.all_to_all(outgoing, 'fsdp', split_axis=0, concat_axis=0, tiled=True)  33.1 us
    psum x1, waiting for transfers between devices, body(): lax.psum(partial_value.astype(jnp.bfloat16), 'tp').astype(jnp.float32)  28.6 us
    ppermute x3, waiting for transfers between devices, mix_squares_over_axis(): ppermute(cards[-1], axis_name=mesh_ax, perm=[(dev_j, (dev_j + 1) % n) for...  25.8 us
    psum x1, blocking collectives, body(): sums, counts = lax.psum((sums, counts), 'fsdp')  21.4 us
    dot_general x1, matrix products, body(): jnp.dot(hidden, down_full, preferred_element_type=jnp.float32)  19.6 us
  transfers between devices with their start and end apart: 9, of which 9 were waited for; matrix products, arithmetic and copies ran while one was open for 2% of the time, Pallas kernels for 0%

profile of v1, /device:TPU:0, one launch (start us, length us, event | category | flops | bytes accessed | tf_op | source)
XLA Modules:
  0.0 727.7 jit_solution(10326600088449746105)
XLA Ops:
  7.2 0.0 copy-start
  7.2 0.0 copy-start.7
  7.2 0.0 copy-start.1
  7.2 0.0 all-gather.4.cloned.1.call-start
  7.2 0.7 all-gather.4.cloned.1.call-update
  7.9 0.0 all-gather.6.cloned.1.call-start
  8.0 0.7 all-gather.6.cloned.1.call-update
  8.7 0.0 all-gather.8.cloned.1.call-start
  8.7 0.7 all-gather.8.cloned.1.call-update
  9.4 0.0 all-reduce.3.cloned.1.call-start
  9.5 0.0 copy-done.7
  9.5 0.1 select_reduce_fusion.2
  9.6 0.0 copy-done.1
  9.6 0.6 gather_fusion.2
  10.3 0.0 copy-done
  10.3 0.6 gather_fusion
  10.9 0.1 broadcast_select_fusion
  11.0 33.1 %all_to_all.23 = bf16[8,32,1024]{2,1,0:T(8,128)(2,1)S(1)} all-to-all(bf16[8,32,1024]{2,1,0:T(8,128)(2,1)S(1)} %broadcast_select_fusion), channel_id=1, replica_groups=mesh['fsdp'=8,'tp'=4] {'fsdp'}, dimensions={0} | all-to-all | bytes 1048576 | tf_op jit(solution)/shard_map/all_to_all | solution.py:49
  44.1 0.0 collective-permute-start
  44.1 8.6 %collective-permute-done = bf16[8,32,1024]{2,1,0:T(8,128)(2,1)S(1)} collective-permute-done((bf16[8,32,1024]{2,1,0:T(8,128)(2,1)S(1)}, bf16[8,32,1024]{2,1,0:T(8,128)(2,1)S(1)}, u32[]{:S(2)}, u32[]{:S(2)}) %collective-permute-start) | collective-permute-done | bytes 524320 | tf_op jit(solution)/shard_map/ppermute | solution.py:16
  52.7 0.0 collective-permute-start.1
  52.7 8.6 %collective-permute-done.1 = bf16[8,32,1024]{2,1,0:T(8,128)(2,1)S(1)} collective-permute-done((bf16[8,32,1024]{2,1,0:T(8,128)(2,1)S(1)}, bf16[8,32,1024]{2,1,0:T(8,128)(2,1)S(1)}, u32[]{:S(2)}, u32[]{:S(2)}) %collective-permute-start.1) | collective-permute-done | bytes 524320 | tf_op jit(solution)/shard_map/ppermute | solution.py:16
  61.3 0.0 collective-permute-start.2
  61.3 8.6 %collective-permute-done.2 = bf16[8,32,1024]{2,1,0:T(8,128)(2,1)S(1)} collective-permute-done((bf16[8,32,1024]{2,1,0:T(8,128)(2,1)S(1)}, bf16[8,32,1024]{2,1,0:T(8,128)(2,1)S(1)}, u32[]{:S(2)}, u32[]{:S(2)}) %collective-permute-start.2) | collective-permute-done | bytes 524320 | tf_op jit(solution)/shard_map/ppermute | solution.py:16
  70.0 0.0 copy-start.4
  70.3 0.0 copy-start.3
  70.3 2.1 copy-done.3
  72.4 0.5 fusion
  72.9 0.1 rsqrt.17
  73.0 0.0 copy-done.4
  73.0 2.2 fusion.2
  75.2 145.7 %all-gather.4.cloned.1.call-done = bf16[4096,1792]{1,0:T(8,128)(2,1)} async-done(((bf16[512,1792]{1,0:T(8,128)(2,1)}), bf16[4096,1792]{1,0:T(8,128)(2,1)}) %all-gather.4.cloned.1.call-update) | async-done | bytes 14680080 | tf_op jit(solution)/shard_map/all_gather | solution.py:63
  220.9 8.5 %fusion.6 = f32[256,1792]{1,0:T(8,128)} fusion(bf16[256,4096]{1,0:T(8,128)(2,1)S(1)} %fusion.2, bf16[4096,1792]{1,0:T(8,128)(2,1)} %all-gather.4.cloned.1.call-done), kind=kOutput, calls=%fused_computation.44 | convolution fusion | flops 3758096384 | bytes 18612224 | tf_op jit(solution)/shard_map/dot_general | solution.py:67
  229.4 0.0 copy-start.2
  229.4 0.0 copy-start.5
  229.4 0.0 copy-start.6
  229.4 193.9 %all-gather.6.cloned.1.call-done = bf16[4096,1792]{1,0:T(8,128)(2,1)} async-done(((bf16[512,1792]{1,0:T(8,128)(2,1)}), bf16[4096,1792]{1,0:T(8,128)(2,1)}) %all-gather.6.cloned.1.call-update) | async-done | bytes 14680080 | tf_op jit(solution)/shard_map/all_gather | solution.py:64
  423.3 202.4 %all-gather.8.cloned.1.call-done = bf16[1792,4096]{1,0:T(8,128)(2,1)} async-done(((bf16[1792,512]{1,0:T(8,128)(2,1)}), bf16[1792,4096]{1,0:T(8,128)(2,1)}) %all-gather.8.cloned.1.call-update) | async-done | bytes 14680080 | tf_op jit(solution)/shard_map/all_gather | solution.py:65
  625.8 19.6 %convolution_convert_fusion = bf16[256,4096]{1,0:T(8,128)(2,1)} fusion(bf16[1792,4096]{1,0:T(8,128)(2,1)} %all-gather.8.cloned.1.call-done, bf16[256,4096]{1,0:T(8,128)(2,1)S(1)} %fusion.2, bf16[4096,1792]{1,0:T(8,128)(2,1)} %all-gather.6.cloned.1.call-done, f32[256,1792]{1,0:T(8,128)} %fusion.6), kind=kOutput, calls=%fused_computation.3 | convolution fusion | flops 7519993856 | bytes 35389440 | tf_op jit(solution)/shard_map/dot_general | solution.py:70
  645.4 0.0 all-reduce.3.cloned.1.call-update
  645.4 0.0 copy-done.2
  645.4 0.6 gather_fusion.1
  646.1 0.7 copy.16
  646.8 3.3 all-to-all-start
  650.1 0.7 copy.17
  650.8 0.0 copy-done.5
  650.8 0.0 copy-done.6
  650.8 5.7 all-to-all-done
  656.5 3.3 all-to-all-start.2
  659.8 0.2 reduce.1
  660.0 6.2 all-to-all-done.2
  666.2 0.2 reduce.3
  666.4 0.1 convert_reduce_fusion.1
  666.6 28.6 %all-reduce.3.cloned.1.call-done = bf16[256,4096]{1,0:T(8,128)(2,1)} async-done(((bf16[256,4096]{1,0:T(8,128)(2,1)}), bf16[256,4096]{1,0:T(8,128)(2,1)}) %all-reduce.3.cloned.1.call-update) | async-done | bytes 2097168 | tf_op jit(solution)/shard_map/psum | solution.py:72
  695.1 3.3 multiply_reduce_fusion
  698.4 0.1 mul.87
  698.5 0.2 select_reduce_fusion.1
  698.7 0.5 bitcast_divide_fusion
  699.2 0.1 convert_reduce_fusion
  699.3 21.4 %all-reduce = (f32[8]{0:T(128)S(1)}, f32[8]{0:T(128)S(1)}) all-reduce(f32[8]{0:T(128)S(1)} %get-tuple-element.6, f32[8]{0:T(128)S(1)} %get-tuple-element.5), channel_id=1, replica_groups=mesh['fsdp'=8,'tp'=4] {'fsdp'}, use_global_device_ids=true, to_apply=%region_7.9 | all-reduce | flops 16 | bytes 128 | tf_op jit(solution)/shard_map/psum | solution.py:84
  720.7 0.5 div.42
  (18 shorter events, 0.4 us)
Async XLA Ops:
  7.2 3.1 copy-start
  7.2 2.3 copy-start.7
  7.2 2.4 copy-start.1
  7.2 213.7 %all-gather.4.cloned.1.call-start = ((), (), s32[]{:S(2)}) async-start(), calls=%async_computation.3 | async-start | bytes 16515072 | tf_op jit(solution)/shard_map/all_gather | solution.py:63
  7.9 415.4 %all-gather.6.cloned.1.call-start = ((), (), s32[]{:S(2)}) async-start(), calls=%async_computation.4 | async-start | bytes 16515072 | tf_op jit(solution)/shard_map/all_gather | solution.py:64
  8.7 617.1 %all-gather.8.cloned.1.call-start = ((), (), s32[]{:S(2)}) async-start(), calls=%async_computation.5 | async-start | bytes 16515072 | tf_op jit(solution)/shard_map/all_gather | solution.py:65
  9.4 685.7 %all-reduce.3.cloned.1.call-start = ((), (), s32[]{:S(2)}) async-start(), calls=%async_computation.6 | async-start | bytes 4194304 | tf_op jit(solution)/shard_map/psum | solution.py:72
  44.1 8.6 %collective-permute-start = (bf16[8,32,1024]{2,1,0:T(8,128)(2,1)S(1)}, bf16[8,32,1024]{2,1,0:T(8,128)(2,1)S(1)}, u32[]{:S(2)}, u32[]{:S(2)}) collective-permute-start(bf16[8,32,1024]{2,1,0:T(8,128)(2,1)S(1)} %all_to_all.23), channel_id=1, source_target_pairs={{0,1},{1,2},{2,3},{3,0},{4,5},{5,6},{6,7},{7,4},{8,9},{9,10},{10,1... | collective-permute-start | bytes 1572872 | tf_op jit(solution)/shard_map/ppermute | solution.py:16
  52.7 8.6 %collective-permute-start.1 = (bf16[8,32,1024]{2,1,0:T(8,128)(2,1)S(1)}, bf16[8,32,1024]{2,1,0:T(8,128)(2,1)S(1)}, u32[]{:S(2)}, u32[]{:S(2)}) collective-permute-start(bf16[8,32,1024]{2,1,0:T(8,128)(2,1)S(1)} %collective-permute-done), channel_id=1, source_target_pairs={{0,1},{1,2},{2,3},{3,0},{4,5},{5,6},{6,7},{7,4},{8,9},{9,10},{10,1... | collective-permute-start | bytes 1572872 | tf_op jit(solution)/shard_map/ppermute | solution.py:16
  61.3 8.6 %collective-permute-start.2 = (bf16[8,32,1024]{2,1,0:T(8,128)(2,1)S(1)}, bf16[8,32,1024]{2,1,0:T(8,128)(2,1)S(1)}, u32[]{:S(2)}, u32[]{:S(2)}) collective-permute-start(bf16[8,32,1024]{2,1,0:T(8,128)(2,1)S(1)} %collective-permute-done.1), channel_id=1, source_target_pairs={{0,1},{1,2},{2,3},{3,0},{4,5},{5,6},{6,7},{7,4},{8,9},{9,10},{10,1... | collective-permute-start | bytes 1572872 | tf_op jit(solution)/shard_map/ppermute | solution.py:16
  70.0 3.0 copy-start.4
  70.3 2.1 copy-start.3
  229.4 416.0 %copy-start.2 = (s32[1,8]{1,0:T(1,128)S(1)}, s32[1,8]{1,0:T(1,128)}, u32[]{:S(2)}) copy-start(s32[1,8]{1,0:T(1,128)} %param.14) | copy-start | bytes 100
  229.4 421.4 %copy-start.5 = (f32[4096]{0:T(1024)S(1)}, f32[4096]{0:T(1024)}, u32[]{:S(2)}) copy-start(f32[4096]{0:T(1024)} %param.20) | copy-start | bytes 49156
  229.4 421.4 %copy-start.6 = (f32[4096]{0:T(1024)S(1)}, f32[4096]{0:T(1024)}, u32[]{:S(2)}) copy-start(f32[4096]{0:T(1024)} %param.21) | copy-start | bytes 49156
  646.8 9.7 %all-to-all-start = ((s32[8,1,1]{2,1,0:T(1,128)}), s32[8,1,1]{2,1,0:T(1,128)S(1)}, u32[]{:S(2)}, u32[]{:S(2)}) async-start(s32[8,1,1]{2,1,0:T(1,128)} %copy.16), calls=%async_computation | async-start | bytes 8192 | tf_op jit(solution)/shard_map/all_to_all | solution.py:50
  656.5 9.7 %all-to-all-start.2 = ((s32[8,1,1]{2,1,0:T(1,128)}), s32[8,1,1]{2,1,0:T(1,128)S(1)}, u32[]{:S(2)}, u32[]{:S(2)}) async-start(s32[8,1,1]{2,1,0:T(1,128)} %copy.17), calls=%async_computation.2 | async-start | bytes 8192 | tf_op jit(solution)/shard_map/all_to_all | solution.py:51
Sparse Core Ops, SparseCore 0:
  10.2 210.6 all-gather.3
  223.1 200.1 all-gather.5
  425.4 200.3 all-gather.7
  645.6 49.5 all-reduce.2
